TPU v7x, 32 devices: a whole 2x2x4 slice. The times are simulated.
32 devices in a mesh: row: 8 (over y, x, core), col: 4 (over z).
Axes of the slice: x: 2, y: 2, z: 4, core: 2. Of those that a mesh axis runs over, the one named last changes fastest.
Arguments:
- iterate_t: bfloat16 [8, 4, 1024, 32768], P(None, 'col', None, 'row'), may hold values from -0.03125 to 0.03125
- vectors: bfloat16 [32768, 256], P(('row', 'col')), may hold values from -6 to 6
- old_factor_t: bfloat16 [512, 32768], P('col', 'row'), may hold values from -5 to 5
Outputs:
- panel: float32 [32768, 256], P(('row', 'col'))
- basis: float32 [768, 32768], P('col', 'row')
All inputs are finite; a program needn't handle non-finite values.
Results may differ from a plain program's by a relative error of at most 0.0013.
Values may be sent and summed in bfloat16 or wider, within the bound.
No kernel may reach another device: no remote copies, remote signals or barrier semaphores. Data moves between devices by JAX's collectives and lax.ppermute only.
A program may use at most 192 MiB of HBM per device.

v0:
```python
import jax
import jax.numpy as jnp
from jax import lax
from jax.sharding import PartitionSpec as P

NSTATE = 32768


def body(iterate_t, vectors, old_factor_t):
    flat_iterate = iterate_t.reshape(-1, iterate_t.shape[-1])
    highest = lax.Precision.HIGHEST

    def apply_iterate(vector):
        gathered = lax.all_gather(vector, "row", axis=0, tiled=True)
        return lax.psum_scatter(
            lax.dot_general(
                flat_iterate, gathered, (((0,), (0,)), ((), ())), preferred_element_type=jnp.float32
            ),
            "col",
            scatter_dimension=0,
            tiled=True,
        )

    first_full = apply_iterate(vectors)
    second = apply_iterate(first_full.astype(jnp.bfloat16)).astype(jnp.bfloat16)
    panel = 1.5 * first_full - 0.5 * apply_iterate(second)
    old_gathered = lax.all_gather(old_factor_t, "col", axis=0, tiled=True)
    panel_gathered = lax.all_gather(panel, "col", axis=0, tiled=True)
    old_full = old_gathered.astype(jnp.float32)
    scale_gram = 1.0 / NSTATE
    column = lax.axis_index("col")
    groups = lax.axis_size("col")
    old_old = lax.dot_general(
        old_gathered, old_gathered, (((1,), (1,)), ((), ())), preferred_element_type=jnp.float32
    )
    old_panel = jnp.dot(old_full, panel_gathered, precision=highest)
    panel_panel = lax.dot_general(
        panel_gathered, panel_gathered, (((0,), (0,)), ((), ())), precision=highest
    )
    local_gram = (
        jnp.concatenate(
            [
                jnp.concatenate([old_old, old_panel], 1),
                jnp.concatenate([old_panel.T, panel_panel], 1),
            ],
            0,
        )
        * scale_gram
    )
    gram = lax.psum(local_gram, "row")
    lower_factor = jnp.linalg.cholesky(gram)
    identity = jnp.eye(gram.shape[0], dtype=jnp.float32)
    inverse = jax.scipy.linalg.solve_triangular(lower_factor, identity, lower=True)
    basis_share = gram.shape[0] // groups
    inverse_rows = lax.dynamic_slice_in_dim(inverse, column * basis_share, basis_share, 0)
    old_count = old_gathered.shape[0]
    basis = jnp.dot(inverse_rows[:, :old_count], old_full, precision=highest)
    basis = basis + lax.dot_general(
        inverse_rows[:, old_count:], panel_gathered, (((1,), (1,)), ((), ())), precision=highest
    )
    return (panel, basis)


def solution(mesh):
    return jax.shard_map(
        body,
        mesh=mesh,
        in_specs=(P(None, "col", None, "row"), P(("row", "col"), None), P("col", "row")),
        out_specs=(P(("row", "col"), None), P("col", "row")),
        check_vma=False,
    )
```

profile of v0, /device:TPU:0, one launch (start us, length us, event | category | flops | bytes accessed | tf_op | source)
XLA Modules:
  0.0 959.2 jit_solution(827991322288170241)
XLA Ops:
  7.9 41.3 %all-gather.6.cloned.1.call-done = bf16[8192,256]{1,0:T(8,128)(2,1)} async-done(((bf16[1024,256]{1,0:T(8,128)(2,1)}), bf16[8192,256]{1,0:T(8,128)(2,1)}) %all-gather.6.cloned.1.call-update) | async-done | bytes 4194320 | tf_op jit(solution)/shard_map/all_gather | solution.py:14
  49.2 30.1 %fusion.59 = f32[4096,256]{1,0:T(8,128)} fusion(bf16[8192,4096]{1,0:T(8,128)(2,1)} %bitcast, bf16[8192,256]{1,0:T(8,128)(2,1)} %all-gather.6.cloned.1.call-done), kind=kOutput, calls=%fused_computation.124 | convolution fusion | flops 17179869184 | bytes 75497472 | tf_op jit(solution)/shard_map/dot_general | solution.py:16
  79.4 76.9 %reduce-scatter.4.cloned.1.call-done = f32[1024,256]{1,0:T(8,128)} async-done(((f32[4096,256]{1,0:T(8,128)}), f32[1024,256]{1,0:T(8,128)}) %reduce-scatter.4.cloned.1.call-update) | async-done | bytes 1048592 | tf_op jit(solution)/shard_map/reduce_scatter | solution.py:15
  158.6 37.2 %all-gather.8.cloned.1.call-done = bf16[8192,256]{1,0:T(8,128)(2,1)} async-done(((bf16[1024,256]{1,0:T(8,128)(2,1)}), bf16[8192,256]{1,0:T(8,128)(2,1)}) %all-gather.8.cloned.1.call-update) | async-done | bytes 4194320 | tf_op jit(solution)/shard_map/all_gather | solution.py:14
  195.9 30.1 %convolution_bitcast_fusion.1 = f32[4096,256]{0,1:T(8,128)} fusion(bf16[8192,256]{1,0:T(8,128)(2,1)} %all-gather.8.cloned.1.call-done, bf16[8192,4096]{1,0:T(8,128)(2,1)} %bitcast), kind=kOutput, calls=%fused_computation.3 | convolution fusion | flops 17179869184 | bytes 75497472 | tf_op jit(solution)/shard_map/dot_general | solution.py:16
  226.0 76.9 %reduce-scatter.6.cloned.1.call-done = f32[1024,256]{0,1:T(8,128)} async-done(((f32[4096,256]{0,1:T(8,128)}), f32[1024,256]{0,1:T(8,128)}) %reduce-scatter.6.cloned.1.call-update) | async-done | bytes 1048592 | tf_op jit(solution)/shard_map/reduce_scatter | solution.py:15
  305.1 37.3 %all-gather.10.cloned.1.call-done = bf16[8192,256]{0,1:T(8,128)(2,1)} async-done(((bf16[1024,256]{0,1:T(8,128)(2,1)}), bf16[8192,256]{0,1:T(8,128)(2,1)}) %all-gather.10.cloned.1.call-update) | async-done | bytes 4194320 | tf_op jit(solution)/shard_map/all_gather | solution.py:14
  342.4 35.5 %convolution_bitcast_fusion = f32[4096,256]{1,0:T(8,128)} fusion(bf16[8192,256]{0,1:T(8,128)(2,1)} %all-gather.10.cloned.1.call-done, bf16[8192,4096]{1,0:T(8,128)(2,1)} %bitcast), kind=kOutput, calls=%fused_computation.2 | convolution fusion | flops 17179869184 | bytes 75497472 | tf_op jit(solution)/shard_map/dot_general | solution.py:16
  379.1 75.7 %reduce-scatter.8.cloned.1.call-done = f32[1024,256]{1,0:T(8,128)} async-done(((f32[4096,256]{1,0:T(8,128)}), f32[1024,256]{1,0:T(8,128)}) %reduce-scatter.8.cloned.1.call-update) | async-done | bytes 1048592 | tf_op jit(solution)/shard_map/reduce_scatter | solution.py:15
  457.2 80.5 %all-gather.12.cloned.1.call-done = bf16[512,4096]{1,0:T(8,128)(2,1)} async-done(((bf16[128,4096]{1,0:T(8,128)(2,1)}), bf16[512,4096]{1,0:T(8,128)(2,1)}) %all-gather.12.cloned.1.call-update) | async-done | bytes 4194320 | tf_op jit(solution)/shard_map/all_gather | solution.py:27
  543.5 75.6 %all-gather.14.cloned.1.call-done = f32[4096,256]{1,0:T(8,128)} async-done(((f32[1024,256]{1,0:T(8,128)}), f32[4096,256]{1,0:T(8,128)}) %all-gather.14.cloned.1.call-update) | async-done | bytes 4194320 | tf_op jit(solution)/shard_map/all_gather | solution.py:28
  619.1 9.8 %fusion.61 = f32[256,512]{1,0:T(8,128)S(1)} fusion(f32[4096,256]{1,0:T(8,128)} %all-gather.14.cloned.1.call-done, bf16[512,4096]{1,0:T(8,128)(2,1)} %all-gather.12.cloned.1.call-done), kind=kOutput, calls=%fused_computation.126 | convolution fusion | flops 6442450944 | bytes 8912896 | tf_op jit(solution)/shard_map/dot_general | solution.py:36
  629.1 10.2 %fusion.62 = f32[256,256]{0,1:T(8,128)S(1)} fusion(f32[4096,256]{1,0:T(8,128)} %all-gather.14.cloned.1.call-done), kind=kOutput, calls=%fused_computation.127 | convolution fusion | flops 3221225472 | bytes 4456448 | tf_op jit(solution)/shard_map/dot_general | solution.py:37
  642.8 59.8 %all-reduce.3.cloned.1.call-done = f32[768,768]{0,1:T(8,128)} async-done(((f32[768,768]{0,1:T(8,128)}), f32[768,768]{0,1:T(8,128)}) %all-reduce.3.cloned.1.call-update) | async-done | bytes 2359312 | tf_op jit(solution)/shard_map/psum | solution.py:50
  709.4 11.7 %cholesky.165 = f32[128,128]{1,0:T(8,128)S(1)} custom-call(f32[128,128]{1,0:T(8,128)S(1)} %cholesky.424), custom_call_target="Cholesky" | custom-call | tf_op jit(solution)/shard_map/jit(cholesky)/cholesky | solution.py:51
  721.1 9.8 %custom-call.47 = f32[1,128,128]{1,2,0:T(8,128)S(1)} custom-call(f32[1,128,128]{2,1,0:T(8,128)S(1)} %get-tuple-element.45), custom_call_target="InvertDiagBlocksLowerTriangular" | custom-call | tf_op jit(solution)/shard_map/jit(cholesky)/cholesky | solution.py:51
  733.9 11.7 %cholesky.188 = f32[128,128]{1,0:T(8,128)S(1)} custom-call(f32[128,128]{1,0:T(8,128)S(1)} %cholesky.428), custom_call_target="Cholesky" | custom-call | tf_op jit(solution)/shard_map/jit(cholesky)/cholesky | solution.py:51
  745.7 10.2 %custom-call.48 = f32[1,128,128]{1,2,0:T(8,128)S(1)} custom-call(f32[1,128,128]{2,1,0:T(8,128)S(1)} %get-tuple-element.42), custom_call_target="InvertDiagBlocksLowerTriangular" | custom-call | tf_op jit(solution)/shard_map/jit(cholesky)/cholesky | solution.py:51
  757.8 11.7 %cholesky.354 = f32[128,128]{1,0:T(8,128)S(1)} custom-call(f32[128,128]{1,0:T(8,128)S(1)} %cholesky.433), custom_call_target="Cholesky" | custom-call | tf_op jit(solution)/shard_map/jit(cholesky)/cholesky | solution.py:51
  781.9 11.9 %cholesky.373 = f32[128,128]{1,0:T(8,128)S(1)} custom-call(f32[128,128]{1,0:T(8,128)S(1)} %cholesky.438), custom_call_target="Cholesky" | custom-call | tf_op jit(solution)/shard_map/jit(cholesky)/cholesky | solution.py:51
  806.1 11.7 %cholesky.392 = f32[128,128]{1,0:T(8,128)S(1)} custom-call(f32[128,128]{1,0:T(8,128)S(1)} %cholesky.443), custom_call_target="Cholesky" | custom-call | tf_op jit(solution)/shard_map/jit(cholesky)/cholesky | solution.py:51
  829.8 11.7 %cholesky.410 = f32[128,128]{1,0:T(8,128)S(1)} custom-call(f32[128,128]{1,0:T(8,128)S(1)} %convolution_subtract_fusion.8), custom_call_target="Cholesky" | custom-call | tf_op jit(solution)/shard_map/jit(cholesky)/cholesky | solution.py:51
  848.3 21.1 %while.1 = (s32[]{:T(128)}, f32[768,768]{1,0:T(8,128)}, s32[6,2]{0,1:T(2,128)S(1)}, f32[6,128,128]{2,1,0:T(8,128)}, s32[]{:T(128)}) while((s32[]{:T(128)}, f32[768,768]{1,0:T(8,128)}, s32[6,2]{0,1:T(2,128)S(1)}, f32[6,128,128]{2,1,0:T(8,128)}, s32[]{:T(128)}) %tuple.44), condition=%wide.while_cond, body=%wide.while_body.sunk | while | flops 2 | bytes 132705 | solution.py:53
  869.4 60.6 %custom-call.52 = f32[6,128,128]{1,2,0:T(8,128)} custom-call(f32[6,128,128]{2,1,0:T(8,128)} %get-tuple-element.9), custom_call_target="InvertDiagBlocksLowerTriangular" | custom-call | tf_op jit(solution)/shard_map/jit(_solve_triangular)/triangular_solve | solution.py:53
  (107 shorter events, 113.0 us)
Async XLA Ops:
  7.2 42.0 %all-gather.6.cloned.1.call-start = ((), (), s32[]{:S(2)}) async-start(), calls=%async_computation.3 | async-start | bytes 4718592 | tf_op jit(solution)/shard_map/all_gather | solution.py:14
  7.9 148.4 %reduce-scatter.4.cloned.1.call-start = ((), (), s32[]{:S(2)}) async-start(), calls=%async_computation.4 | async-start | bytes 5242880 | tf_op jit(solution)/shard_map/reduce_scatter | solution.py:15
  79.3 116.5 %all-gather.8.cloned.1.call-start = ((), (), s32[]{:S(2)}) async-start(), calls=%async_computation.5 | async-start | bytes 4718592 | tf_op jit(solution)/shard_map/all_gather | solution.py:14
  158.4 144.6 %reduce-scatter.6.cloned.1.call-start = ((), (), s32[]{:S(2)}) async-start(), calls=%async_computation.6 | async-start | bytes 5242880 | tf_op jit(solution)/shard_map/reduce_scatter | solution.py:15
  226.0 116.4 %all-gather.10.cloned.1.call-start = ((), (), s32[]{:S(2)}) async-start(), calls=%async_computation.7 | async-start | bytes 4718592 | tf_op jit(solution)/shard_map/all_gather | solution.py:14
  305.1 149.8 %reduce-scatter.8.cloned.1.call-start = ((), (), s32[]{:S(2)}) async-start(), calls=%async_computation.8 | async-start | bytes 5242880 | tf_op jit(solution)/shard_map/reduce_scatter | solution.py:15
  377.9 77.0 %copy-start.5 = (f32[1024,256]{1,0:T(8,128)S(1)}, f32[1024,256]{1,0:T(8,128)}, u32[]{:S(2)}) copy-start(f32[1024,256]{1,0:T(8,128)} %reduce-scatter.4.cloned.1.call-done) | copy-start | bytes 3145732
  377.9 159.8 %all-gather.12.cloned.1.call-start = ((), (), s32[]{:S(2)}) async-start(), calls=%async_computation.9 | async-start | bytes 5242880 | tf_op jit(solution)/shard_map/all_gather | solution.py:27
  378.6 240.4 %all-gather.14.cloned.1.call-start = ((), (), s32[]{:S(2)}) async-start(), calls=%async_computation.10 | async-start | bytes 5242880 | tf_op jit(solution)/shard_map/all_gather | solution.py:28
  457.2 245.5 %all-reduce.3.cloned.1.call-start = ((), (), s32[]{:S(2)}) async-start(), calls=%async_computation.11 | async-start | bytes 4718592 | tf_op jit(solution)/shard_map/psum | solution.py:50
  702.6 3.4 copy-start.2
  708.0 1.4 copy-start.4
  848.3 85.0 %copy-start.3 = (f32[768,768]{1,0:T(8,128)S(1)}, f32[768,768]{1,0:T(8,128)}, u32[]{:S(2)}) copy-start(f32[768,768]{1,0:T(8,128)} %fusion.20) | copy-start | bytes 7077892
  930.0 2.8 copy-start.6
  939.7 3.6 copy-start.1
  943.4 2.8 copy-start
Sparse Core Ops, SparseCore 0:
  9.9 39.2 all-gather.5
  79.4 76.7 reduce-scatter.3
  158.8 37.0 all-gather.7
  226.1 76.7 reduce-scatter.5
  305.3 37.0 all-gather.9
  378.0 76.7 reduce-scatter.7
  456.4 81.2 all-gather.11
  539.8 79.2 all-gather.13
  641.1 61.4 all-reduce.2
where the time goes:
time: 965 us; the launch traced here: 959 us
  waiting for transfers between devices  563 us (58%)
  other arithmetic  197 us (20%)
  matrix products  154 us (16%)
  local copies, waits for them, and re-layouts  26.2 us (3%)
  between operations  18.4 us (2%)
    reduce_scatter x3, waiting for transfers between devices, apply_iterate(): lax.psum_scatter(lax.dot_general(flat_iterate, gathered, (((0,), (0,)), (...  230 us
    another operation x22, other arithmetic, body(): lower_factor = jnp.linalg.cholesky(gram)  123 us
    all_gather x3, waiting for transfers between devices, apply_iterate(): gathered = lax.all_gather(vector, 'row', axis=0, tiled=True)  116 us
    dot_general x3, matrix products, apply_iterate(): lax.dot_general(flat_iterate, gathered, (((0,), (0,)), ((), ())), preferr...  95.7 us
    all_gather x1, waiting for transfers between devices, body(): old_gathered = lax.all_gather(old_factor_t, 'col', axis=0, tiled=True)  80.5 us
    all_gather x1, waiting for transfers between devices, body(): panel_gathered = lax.all_gather(panel, 'col', axis=0, tiled=True)  75.6 us
    another operation x3, other arithmetic, body(): jax.scipy.linalg.solve_triangular(lower_factor, identity, lower=True)  62.2 us
    psum x1, waiting for transfers between devices, body(): gram = lax.psum(local_gram, 'row')  59.8 us
  transfers between devices with their start and end apart: 9, of which 9 were waited for; matrix products, arithmetic and copies ran while one was open for 1% of the time, Pallas kernels for 0%

commit v1 on v0

--- a/solution.py
+++ b/solution.py
@@ -47,7 +47,8 @@
         )
         * scale_gram
     )
-    gram = lax.psum(local_gram, "row")
+    terms = lax.all_gather(local_gram, "row", axis=0, tiled=False)
+    gram = terms.sum(axis=0)
     lower_factor = jnp.linalg.cholesky(gram)
     identity = jnp.eye(gram.shape[0], dtype=jnp.float32)
     inverse = jax.scipy.linalg.solve_triangular(lower_factor, identity, lower=True)

time: 965 us -> 1010 us (1.047)
  waiting for transfers between devices: 563 us -> 598 us
    all_gather x0 -> x1, waiting for transfers between devices: none -> 95.5 us  [body(): terms = lax.all_gather(local_gram, 'row', axis=0, tiled=False)]
    psum x1 -> x0, waiting for transfers between devices: 59.8 us -> none  [body(): gram = lax.psum(local_gram, 'row')]
where the time goes in v1:
time: 1010 us; the launch traced here: 1000 us
  waiting for transfers between devices  598 us (59%)
  other arithmetic  204 us (20%)
  matrix products  154 us (15%)
  local copies, waits for them, and re-layouts  26.5 us (3%)
  between operations  18.3 us (2%)
    reduce_scatter x3, waiting for transfers between devices, apply_iterate(): lax.psum_scatter(lax.dot_general(flat_iterate, gathered, (((0,), (0,)), (...  229 us
    another operation x22, other arithmetic, body(): lower_factor = jnp.linalg.cholesky(gram)  123 us
    all_gather x3, waiting for transfers between devices, apply_iterate(): gathered = lax.all_gather(vector, 'row', axis=0, tiled=True)  116 us
    dot_general x3, matrix products, apply_iterate(): lax.dot_general(flat_iterate, gathered, (((0,), (0,)), ((), ())), preferr...  95.7 us
    all_gather x1, waiting for transfers between devices, body(): terms = lax.all_gather(local_gram, 'row', axis=0, tiled=False)  95.5 us
    all_gather x1, waiting for transfers between devices, body(): old_gathered = lax.all_gather(old_factor_t, 'col', axis=0, tiled=True)  80.4 us
    all_gather x1, waiting for transfers between devices, body(): panel_gathered = lax.all_gather(panel, 'col', axis=0, tiled=True)  75.5 us
    another operation x3, other arithmetic, body(): jax.scipy.linalg.solve_triangular(lower_factor, identity, lower=True)  62.2 us
  transfers between devices with their start and end apart: 9, of which 9 were waited for; matrix products, arithmetic and copies ran while one was open for 1% of the time, Pallas kernels for 0%

profile of v1, /device:TPU:0, one launch (start us, length us, event | category | flops | bytes accessed | tf_op | source)
XLA Modules:
  0.0 1001.6 jit_solution(590455827793759677)
XLA Ops:
  7.9 41.3 %all-gather.7.cloned.1.call-done = bf16[8192,256]{1,0:T(8,128)(2,1)} async-done(((bf16[1024,256]{1,0:T(8,128)(2,1)}), bf16[8192,256]{1,0:T(8,128)(2,1)}) %all-gather.7.cloned.1.call-update) | async-done | bytes 4194320 | tf_op jit(solution)/shard_map/all_gather | solution.py:14
  49.2 30.1 %fusion.59 = f32[4096,256]{1,0:T(8,128)} fusion(bf16[8192,4096]{1,0:T(8,128)(2,1)} %bitcast, bf16[8192,256]{1,0:T(8,128)(2,1)} %all-gather.7.cloned.1.call-done), kind=kOutput, calls=%fused_computation.126 | convolution fusion | flops 17179869184 | bytes 75497472 | tf_op jit(solution)/shard_map/dot_general | solution.py:16
  79.4 76.9 %reduce-scatter.4.cloned.1.call-done = f32[1024,256]{1,0:T(8,128)} async-done(((f32[4096,256]{1,0:T(8,128)}), f32[1024,256]{1,0:T(8,128)}) %reduce-scatter.4.cloned.1.call-update) | async-done | bytes 1048592 | tf_op jit(solution)/shard_map/reduce_scatter | solution.py:15
  158.6 37.2 %all-gather.9.cloned.1.call-done = bf16[8192,256]{1,0:T(8,128)(2,1)} async-done(((bf16[1024,256]{1,0:T(8,128)(2,1)}), bf16[8192,256]{1,0:T(8,128)(2,1)}) %all-gather.9.cloned.1.call-update) | async-done | bytes 4194320 | tf_op jit(solution)/shard_map/all_gather | solution.py:14
  195.9 30.1 %convolution_bitcast_fusion.1 = f32[4096,256]{0,1:T(8,128)} fusion(bf16[8192,256]{1,0:T(8,128)(2,1)} %all-gather.9.cloned.1.call-done, bf16[8192,4096]{1,0:T(8,128)(2,1)} %bitcast), kind=kOutput, calls=%fused_computation.3 | convolution fusion | flops 17179869184 | bytes 75497472 | tf_op jit(solution)/shard_map/dot_general | solution.py:16
  226.0 76.9 %reduce-scatter.6.cloned.1.call-done = f32[1024,256]{0,1:T(8,128)} async-done(((f32[4096,256]{0,1:T(8,128)}), f32[1024,256]{0,1:T(8,128)}) %reduce-scatter.6.cloned.1.call-update) | async-done | bytes 1048592 | tf_op jit(solution)/shard_map/reduce_scatter | solution.py:15
  305.1 37.3 %all-gather.11.cloned.1.call-done = bf16[8192,256]{0,1:T(8,128)(2,1)} async-done(((bf16[1024,256]{0,1:T(8,128)(2,1)}), bf16[8192,256]{0,1:T(8,128)(2,1)}) %all-gather.11.cloned.1.call-update) | async-done | bytes 4194320 | tf_op jit(solution)/shard_map/all_gather | solution.py:14
  342.4 35.5 %convolution_bitcast_fusion = f32[4096,256]{1,0:T(8,128)} fusion(bf16[8192,256]{0,1:T(8,128)(2,1)} %all-gather.11.cloned.1.call-done, bf16[8192,4096]{1,0:T(8,128)(2,1)} %bitcast), kind=kOutput, calls=%fused_computation.2 | convolution fusion | flops 17179869184 | bytes 75497472 | tf_op jit(solution)/shard_map/dot_general | solution.py:16
  379.1 75.7 %reduce-scatter.8.cloned.1.call-done = f32[1024,256]{1,0:T(8,128)} async-done(((f32[4096,256]{1,0:T(8,128)}), f32[1024,256]{1,0:T(8,128)}) %reduce-scatter.8.cloned.1.call-update) | async-done | bytes 1048592 | tf_op jit(solution)/shard_map/reduce_scatter | solution.py:15
  457.2 80.4 %all-gather.13.cloned.1.call-done = bf16[512,4096]{1,0:T(8,128)(2,1)} async-done(((bf16[128,4096]{1,0:T(8,128)(2,1)}), bf16[512,4096]{1,0:T(8,128)(2,1)}) %all-gather.13.cloned.1.call-update) | async-done | bytes 4194320 | tf_op jit(solution)/shard_map/all_gather | solution.py:27
  543.5 75.5 %all-gather.15.cloned.1.call-done = f32[4096,256]{1,0:T(8,128)} async-done(((f32[1024,256]{1,0:T(8,128)}), f32[4096,256]{1,0:T(8,128)}) %all-gather.15.cloned.1.call-update) | async-done | bytes 4194320 | tf_op jit(solution)/shard_map/all_gather | solution.py:28
  619.1 9.8 fusion.61
  629.1 10.2 %fusion.62 = f32[256,256]{0,1:T(8,128)S(1)} fusion(f32[4096,256]{1,0:T(8,128)} %all-gather.15.cloned.1.call-done), kind=kOutput, calls=%fused_computation.129 | convolution fusion | flops 3221225472 | bytes 4456448 | tf_op jit(solution)/shard_map/dot_general | solution.py:37
  643.5 95.5 %all-gather.17.cloned.1.call-done = f32[8,768,768]{2,1,0:T(8,128)} async-done(((f32[1,768,768]{2,1,0:T(8,128)}), f32[8,768,768]{2,1,0:T(8,128)}) %all-gather.17.cloned.1.call-update) | async-done | bytes 18874384 | tf_op jit(solution)/shard_map/all_gather | solution.py:50
  752.3 11.7 %cholesky.165 = f32[128,128]{1,0:T(8,128)S(1)} custom-call(f32[128,128]{1,0:T(8,128)S(1)} %cholesky.424), custom_call_target="Cholesky" | custom-call | tf_op jit(solution)/shard_map/jit(cholesky)/cholesky | solution.py:52
  764.2 9.8 custom-call.47
  776.9 11.7 %cholesky.188 = f32[128,128]{1,0:T(8,128)S(1)} custom-call(f32[128,128]{1,0:T(8,128)S(1)} %cholesky.428), custom_call_target="Cholesky" | custom-call | tf_op jit(solution)/shard_map/jit(cholesky)/cholesky | solution.py:52
  788.6 10.2 %custom-call.48 = f32[1,128,128]{1,2,0:T(8,128)S(1)} custom-call(f32[1,128,128]{2,1,0:T(8,128)S(1)} %get-tuple-element.42), custom_call_target="InvertDiagBlocksLowerTriangular" | custom-call | tf_op jit(solution)/shard_map/jit(cholesky)/cholesky | solution.py:52
  800.7 11.7 %cholesky.354 = f32[128,128]{1,0:T(8,128)S(1)} custom-call(f32[128,128]{1,0:T(8,128)S(1)} %cholesky.433), custom_call_target="Cholesky" | custom-call | tf_op jit(solution)/shard_map/jit(cholesky)/cholesky | solution.py:52
  824.8 11.9 %cholesky.373 = f32[128,128]{1,0:T(8,128)S(1)} custom-call(f32[128,128]{1,0:T(8,128)S(1)} %cholesky.438), custom_call_target="Cholesky" | custom-call | tf_op jit(solution)/shard_map/jit(cholesky)/cholesky | solution.py:52
  849.0 11.7 %cholesky.392 = f32[128,128]{1,0:T(8,128)S(1)} custom-call(f32[128,128]{1,0:T(8,128)S(1)} %cholesky.443), custom_call_target="Cholesky" | custom-call | tf_op jit(solution)/shard_map/jit(cholesky)/cholesky | solution.py:52
  872.8 11.7 %cholesky.410 = f32[128,128]{1,0:T(8,128)S(1)} custom-call(f32[128,128]{1,0:T(8,128)S(1)} %convolution_subtract_fusion.8), custom_call_target="Cholesky" | custom-call | tf_op jit(solution)/shard_map/jit(cholesky)/cholesky | solution.py:52
  891.2 20.7 %while.1 = (s32[]{:T(128)}, f32[768,768]{1,0:T(8,128)}, s32[6,2]{0,1:T(2,128)S(1)}, f32[6,128,128]{2,1,0:T(8,128)}, s32[]{:T(128)}) while((s32[]{:T(128)}, f32[768,768]{1,0:T(8,128)}, s32[6,2]{0,1:T(2,128)S(1)}, f32[6,128,128]{2,1,0:T(8,128)}, s32[]{:T(128)}) %tuple.44), condition=%wide.while_cond, body=%wide.while_body.sunk | while | flops 2 | bytes 132705 | solution.py:54
  911.8 60.6 %custom-call.52 = f32[6,128,128]{1,2,0:T(8,128)} custom-call(f32[6,128,128]{2,1,0:T(8,128)} %get-tuple-element.9), custom_call_target="InvertDiagBlocksLowerTriangular" | custom-call | tf_op jit(solution)/shard_map/jit(_solve_triangular)/triangular_solve | solution.py:54
  (109 shorter events, 119.9 us)
Async XLA Ops:
  7.2 42.0 %all-gather.7.cloned.1.call-start = ((), (), s32[]{:S(2)}) async-start(), calls=%async_computation.3 | async-start | bytes 4718592 | tf_op jit(solution)/shard_map/all_gather | solution.py:14
  7.9 148.4 %reduce-scatter.4.cloned.1.call-start = ((), (), s32[]{:S(2)}) async-start(), calls=%async_computation.4 | async-start | bytes 5242880 | tf_op jit(solution)/shard_map/reduce_scatter | solution.py:15
  79.3 116.5 %all-gather.9.cloned.1.call-start = ((), (), s32[]{:S(2)}) async-start(), calls=%async_computation.5 | async-start | bytes 4718592 | tf_op jit(solution)/shard_map/all_gather | solution.py:14
  158.4 144.6 %reduce-scatter.6.cloned.1.call-start = ((), (), s32[]{:S(2)}) async-start(), calls=%async_computation.6 | async-start | bytes 5242880 | tf_op jit(solution)/shard_map/reduce_scatter | solution.py:15
  226.0 116.4 %all-gather.11.cloned.1.call-start = ((), (), s32[]{:S(2)}) async-start(), calls=%async_computation.7 | async-start | bytes 4718592 | tf_op jit(solution)/shard_map/all_gather | solution.py:14
  305.1 149.8 %reduce-scatter.8.cloned.1.call-start = ((), (), s32[]{:S(2)}) async-start(), calls=%async_computation.8 | async-start | bytes 5242880 | tf_op jit(solution)/shard_map/reduce_scatter | solution.py:15
  377.9 77.0 %copy-start.4 = (f32[1024,256]{1,0:T(8,128)S(1)}, f32[1024,256]{1,0:T(8,128)}, u32[]{:S(2)}) copy-start(f32[1024,256]{1,0:T(8,128)} %reduce-scatter.4.cloned.1.call-done) | copy-start | bytes 3145732
  377.9 159.8 %all-gather.13.cloned.1.call-start = ((), (), s32[]{:S(2)}) async-start(), calls=%async_computation.9 | async-start | bytes 5242880 | tf_op jit(solution)/shard_map/all_gather | solution.py:27
  378.6 240.4 %all-gather.15.cloned.1.call-start = ((), (), s32[]{:S(2)}) async-start(), calls=%async_computation.10 | async-start | bytes 5242880 | tf_op jit(solution)/shard_map/all_gather | solution.py:28
  457.2 281.8 %all-gather.17.cloned.1.call-start = ((), (), s32[]{:S(2)}) async-start(), calls=%async_computation.11 | async-start | bytes 21233664 | tf_op jit(solution)/shard_map/all_gather | solution.py:50
  750.9 1.4 copy-start.3
  891.2 84.6 %copy-start.2 = (f32[768,768]{1,0:T(8,128)S(1)}, f32[768,768]{1,0:T(8,128)}, u32[]{:S(2)}) copy-start(f32[768,768]{1,0:T(8,128)} %fusion.20) | copy-start | bytes 7077892
  972.4 2.8 copy-start.5
  982.1 3.6 copy-start.1
  985.8 2.8 copy-start
Sparse Core Ops, SparseCore 0:
  9.9 39.2 all-gather.6
  79.5 76.7 reduce-scatter.3
  158.8 37.0 all-gather.8
  226.1 76.7 reduce-scatter.5
  305.3 37.0 all-gather.10
  378.0 76.7 reduce-scatter.7
  456.4 81.2 all-gather.12
  539.8 79.2 all-gather.14
  641.9 97.0 all-gather.16
